TPU v7x, 32 devices: a whole 2x2x4 slice. The times are simulated.
32 devices in a mesh: grp: 2 (over core), blk: 16 (over z, y, x).
Axes of the slice: x: 2, y: 2, z: 4, core: 2. Of those that a mesh axis runs over, the one named last changes fastest.
Arguments:
- nullspace: float32 [6, 65536], P(None, ('grp', 'blk')), may hold values from -6 to 6
- agg_ids: int32 [65536], P(('grp', 'blk')), may hold values from 0 to 1535
- nbr_index: int32 [8, 65536], P(None, ('grp', 'blk')), may hold values from 0 to 6143
- nbr_weight: float32 [8, 65536], P(None, ('grp', 'blk')), may hold values from -0.25 to 0.25
Outputs:
- factor: float32 [21, 3072], P(None, ('grp', 'blk'))
- spread: float32 [3072], P(('grp', 'blk'))
All inputs are finite; a program needn't handle non-finite values.
Results may differ from a plain program's by a relative error of at most 0.000088.
Values sent between devices are 32-bit elements; how exact they have to be, the bound alone decides.
No kernel may reach another device: no remote copies, remote signals or barrier semaphores. Data moves between devices by JAX's collectives and lax.ppermute only.
A program may use at most 64 MiB of HBM per device.

v0:
```python
import jax
import jax.numpy as jnp
from jax import lax
from jax.sharding import PartitionSpec as P

ROWS_DEV = 2048
AGG_DEV = 96


def with_halo(cells, sides, width):
    for axis, dim in sides:
        count = lax.axis_size(axis)
        ends = count - 1
        head = lax.slice_in_dim(cells, 0, width, axis=dim)
        tail = lax.slice_in_dim(cells, cells.shape[dim] - width, cells.shape[dim], axis=dim)
        cells = jnp.concatenate(
            [
                lax.ppermute(tail, axis, [(i, (i + 1) % count) for i in range(ends)]),
                cells,
                lax.ppermute(head, axis, [((i + 1) % count, i) for i in range(ends)]),
            ],
            axis=dim,
        )
    return cells


def pair_list():
    return [(p, q) for p in range(6) for q in range(p, 6)]


def factorize(packed):
    pairs = pair_list()
    entry = {}
    for idx, (p, q) in enumerate(pairs):
        entry[p, q] = packed[idx]
        entry[q, p] = packed[idx]
    lower = {}
    for j in range(6):
        total = entry[j, j]
        for k in range(j):
            total = total - lower[j, k] * lower[j, k]
        diag = jnp.sqrt(total)
        lower[j, j] = diag
        for i in range(j + 1, 6):
            total = entry[i, j]
            for k in range(j):
                total = total - lower[i, k] * lower[j, k]
            lower[i, j] = total / diag
    factor = jnp.stack([lower[q, p] for p, q in pairs], axis=0)
    diags = jnp.stack([lower[j, j] for j in range(6)], axis=0)
    spread = jnp.log(jnp.max(diags, axis=0)) - jnp.log(jnp.min(diags, axis=0))
    return (factor, spread)


def shards(nullspace, agg_ids, nbr_index, nbr_weight):
    vectors, rows = nullspace.shape
    neighbours = nbr_index.shape[0]
    padded = with_halo(nullspace[None], (("grp", 0),), 1)
    extended = jnp.transpose(padded, (1, 0, 2)).reshape(vectors, 3 * rows)
    ext_cols = jnp.arange(3 * rows, dtype=jnp.int32)
    blocks_blk = lax.axis_size("blk")
    group_aggs = AGG_DEV * blocks_blk
    block_rows = min(512, rows)
    count_blocks = rows // block_rows
    null_blocks = jnp.transpose(nullspace.reshape(vectors, count_blocks, block_rows), (1, 0, 2))
    index_blocks = jnp.transpose(nbr_index.reshape(neighbours, count_blocks, block_rows), (1, 0, 2))
    weight_blocks = jnp.transpose(
        nbr_weight.reshape(neighbours, count_blocks, block_rows), (1, 0, 2)
    )
    id_blocks = agg_ids.reshape(count_blocks, block_rows)
    columns = jnp.arange(group_aggs, dtype=jnp.int32)
    pairs = pair_list()

    def accumulate(total, inputs):
        null_part, index_part, weight_part, id_part = inputs
        mixing = jnp.zeros((block_rows, 3 * rows), jnp.float32)
        for k in range(neighbours):
            mixing = mixing + jnp.where(
                index_part[k][:, None] == ext_cols[None, :], weight_part[k][:, None], 0.0
            )
        nearby = lax.dot_general(
            extended,
            mixing,
            (((1,), (1,)), ((), ())),
            precision=lax.Precision.HIGHEST,
            preferred_element_type=jnp.float32,
        )
        smoothed = null_part - nearby
        terms = jnp.stack([smoothed[p] * smoothed[q] for p, q in pairs], axis=0)
        one_hot = (id_part[:, None] == columns[None, :]).astype(jnp.float32)
        total = total + jnp.dot(
            terms, one_hot, precision=lax.Precision.HIGHEST, preferred_element_type=jnp.float32
        )
        return (total, None)

    start_total = jnp.zeros((len(pairs), group_aggs), jnp.float32)
    partial_gram, _ = lax.scan(
        accumulate, start_total, (null_blocks, index_blocks, weight_blocks, id_blocks)
    )
    whole = lax.psum(partial_gram, "blk")
    offset = lax.axis_index("blk") * AGG_DEV
    mine = lax.dynamic_slice_in_dim(whole, offset, AGG_DEV, 1)
    identity = jnp.array([1.0 if p == q else 0.0 for p, q in pairs], jnp.float32)
    gram = mine * (AGG_DEV / ROWS_DEV) + identity[:, None]
    return factorize(gram)


def solution(mesh):
    return jax.shard_map(
        shards,
        mesh=mesh,
        in_specs=(
            P(None, ("grp", "blk")),
            P(("grp", "blk")),
            P(None, ("grp", "blk")),
            P(None, ("grp", "blk")),
        ),
        out_specs=(P(None, ("grp", "blk")), P(("grp", "blk"))),
        check_vma=False,
    )
```

profile of v0, /device:TPU:0, one launch (start us, length us, event | category | flops | bytes accessed | tf_op | source)
XLA Modules:
  0.0 279.0 jit_solution(1921388014540714053)
XLA Ops:
  7.2 0.0 all-reduce.2.cloned.1.call-start
  7.2 2.4 collective-permute-start
  9.6 1.3 collective-permute-start.1
  10.9 0.7 reshape.96
  11.6 0.0 collective-permute-done
  11.6 1.3 collective-permute-done.1
  13.0 0.9 pad_maximum_fusion
  13.8 0.0 copy-start.1
  13.9 145.3 %while.12 = (s32[]{:T(128)}, f32[21,1536]{1,0:T(8,128)S(1)}, f32[4,6,512]{2,1,0:T(8,128)}, s32[4,8,512]{2,1,0:T(8,128)}, f32[4,8,512]{2,1,0:T(8,128)}, /*index=5...) while((s32[]{:T(128)}, f32[21,1536]{1,0:T(8,128)S(1)}, ...), condition=%wide.region_1.2_spmd.clone.clone, body=%wide.region_0.1_spmd.clone.clone.sunk | while | flops 497889792 | bytes 25895224 | solution.py:97
  13.9 1.0 constant_dynamic-slice_fusion.20
  14.9 1.0 constant_dynamic-slice_fusion.21
  16.0 21.4 %fusion.81 = f32[512,6144]{1,0:T(8,128)S(1)} fusion(f32[512]{0:T(512)S(1)} %bitcast.100, s32[512]{0:T(512)S(1)} %bitcast.108, f32[512]{0:T(512)S(1)} %bitcast.94, s32[512]{0:T(512)S(1)} %bitcast.102, f32[512]{0:T(512)S(1)} %bitcast.95, s32[512]{0:T(512)S(1)} %bitcast.103, f32[512]{0:T(512)S(1)} %bitcast.96, ...), kind=kLoop, calls=%fused_computation.11.clone.clone.clone.clone.clone.1.clone.1 | loop fusion | flops 72351744 | bytes 12615680 | tf_op jit(solution)/shard_map/while/body/eval_jaxpr/dot_general | solution.py:81
  37.4 11.4 %fusion.82 = f32[6,512]{1,0:T(8,128)S(1)} fusion(f32[6,6144]{1,0:T(8,128)S(1)} %get-tuple-element.373, f32[4,6,512]{2,1,0:T(8,128)} %get-tuple-element.370, s32[]{:T(128)} %get-tuple-element.352, f32[512,6144]{1,0:T(8,128)S(1)} %fusion.81), kind=kOutput, calls=%fused_computation.48.clone.2 | convolution fusion | flops 226495488 | bytes 12754948 | tf_op jit(solution)/shard_map/while/body/eval_jaxpr/dot_general | solution.py:81
  48.9 0.1 stack.8
  49.0 1.2 fusion.83
  50.2 1.0 constant_dynamic-slice_fusion.20
  51.2 1.0 constant_dynamic-slice_fusion.21
  52.3 21.4 %fusion.81 = f32[512,6144]{1,0:T(8,128)S(1)} fusion(f32[512]{0:T(512)S(1)} %bitcast.100, s32[512]{0:T(512)S(1)} %bitcast.108, f32[512]{0:T(512)S(1)} %bitcast.94, s32[512]{0:T(512)S(1)} %bitcast.102, f32[512]{0:T(512)S(1)} %bitcast.95, s32[512]{0:T(512)S(1)} %bitcast.103, f32[512]{0:T(512)S(1)} %bitcast.96, ...), kind=kLoop, calls=%fused_computation.11.clone.clone.clone.clone.clone.1.clone.1 | loop fusion | flops 72351744 | bytes 12615680 | tf_op jit(solution)/shard_map/while/body/eval_jaxpr/dot_general | solution.py:81
  73.7 11.4 %fusion.82 = f32[6,512]{1,0:T(8,128)S(1)} fusion(f32[6,6144]{1,0:T(8,128)S(1)} %get-tuple-element.373, f32[4,6,512]{2,1,0:T(8,128)} %get-tuple-element.370, s32[]{:T(128)} %get-tuple-element.352, f32[512,6144]{1,0:T(8,128)S(1)} %fusion.81), kind=kOutput, calls=%fused_computation.48.clone.2 | convolution fusion | flops 226495488 | bytes 12754948 | tf_op jit(solution)/shard_map/while/body/eval_jaxpr/dot_general | solution.py:81
  85.2 0.1 stack.8
  85.3 1.2 fusion.83
  86.5 1.0 constant_dynamic-slice_fusion.20
  87.6 1.0 constant_dynamic-slice_fusion.21
  88.6 21.4 %fusion.81 = f32[512,6144]{1,0:T(8,128)S(1)} fusion(f32[512]{0:T(512)S(1)} %bitcast.100, s32[512]{0:T(512)S(1)} %bitcast.108, f32[512]{0:T(512)S(1)} %bitcast.94, s32[512]{0:T(512)S(1)} %bitcast.102, f32[512]{0:T(512)S(1)} %bitcast.95, s32[512]{0:T(512)S(1)} %bitcast.103, f32[512]{0:T(512)S(1)} %bitcast.96, ...), kind=kLoop, calls=%fused_computation.11.clone.clone.clone.clone.clone.1.clone.1 | loop fusion | flops 72351744 | bytes 12615680 | tf_op jit(solution)/shard_map/while/body/eval_jaxpr/dot_general | solution.py:81
  110.0 11.4 %fusion.82 = f32[6,512]{1,0:T(8,128)S(1)} fusion(f32[6,6144]{1,0:T(8,128)S(1)} %get-tuple-element.373, f32[4,6,512]{2,1,0:T(8,128)} %get-tuple-element.370, s32[]{:T(128)} %get-tuple-element.352, f32[512,6144]{1,0:T(8,128)S(1)} %fusion.81), kind=kOutput, calls=%fused_computation.48.clone.2 | convolution fusion | flops 226495488 | bytes 12754948 | tf_op jit(solution)/shard_map/while/body/eval_jaxpr/dot_general | solution.py:81
  121.5 0.1 stack.8
  121.7 1.2 fusion.83
  122.8 1.0 constant_dynamic-slice_fusion.20
  123.9 1.0 constant_dynamic-slice_fusion.21
  124.9 21.4 %fusion.81 = f32[512,6144]{1,0:T(8,128)S(1)} fusion(f32[512]{0:T(512)S(1)} %bitcast.100, s32[512]{0:T(512)S(1)} %bitcast.108, f32[512]{0:T(512)S(1)} %bitcast.94, s32[512]{0:T(512)S(1)} %bitcast.102, f32[512]{0:T(512)S(1)} %bitcast.95, s32[512]{0:T(512)S(1)} %bitcast.103, f32[512]{0:T(512)S(1)} %bitcast.96, ...), kind=kLoop, calls=%fused_computation.11.clone.clone.clone.clone.clone.1.clone.1 | loop fusion | flops 72351744 | bytes 12615680 | tf_op jit(solution)/shard_map/while/body/eval_jaxpr/dot_general | solution.py:81
  146.4 11.4 %fusion.82 = f32[6,512]{1,0:T(8,128)S(1)} fusion(f32[6,6144]{1,0:T(8,128)S(1)} %get-tuple-element.373, f32[4,6,512]{2,1,0:T(8,128)} %get-tuple-element.370, s32[]{:T(128)} %get-tuple-element.352, f32[512,6144]{1,0:T(8,128)S(1)} %fusion.81), kind=kOutput, calls=%fused_computation.48.clone.2 | convolution fusion | flops 226495488 | bytes 12754948 | tf_op jit(solution)/shard_map/while/body/eval_jaxpr/dot_general | solution.py:81
  157.9 0.1 stack.8
  158.0 1.2 fusion.83
  159.2 0.0 copy-start
  159.2 0.6 copy-done
  159.8 0.0 all-reduce.2.cloned.1.call-update
  159.9 109.0 %all-reduce.2.cloned.1.call-done = f32[21,1536]{1,0:T(8,128)} async-done(((f32[21,1536]{1,0:T(8,128)}), f32[21,1536]{1,0:T(8,128)}) %all-reduce.2.cloned.1.call-update) | async-done | bytes 129040 | tf_op jit(solution)/shard_map/psum | solution.py:100
  268.8 0.0 copy-done.1
  268.8 0.8 multiply_add_fusion
  269.7 0.6 subtract_bitcast_fusion
  270.3 1.8 stack.4
  (17 shorter events, 0.3 us)
Async XLA Ops:
  7.2 261.6 %all-reduce.2.cloned.1.call-start = ((), (), s32[]{:S(2)}) async-start(), calls=%async_computation | async-start | bytes 294912 | tf_op jit(solution)/shard_map/psum | solution.py:100
  7.2 4.4 %collective-permute-start = (f32[1,6,2048]{2,1,0:T(8,128)}, f32[1,6,2048]{2,1,0:T(8,128)S(1)}, u32[]{:S(2)}, u32[]{:S(2)}) collective-permute-start(f32[1,6,2048]{2,1,0:T(8,128)} %bitcast.89), channel_id=1, source_target_pairs={{0,16},{1,17},{2,18},{3,19},{4,20},{5,21},{6,22},{7,23},{8,24},{9,... | collective-permute-start | bytes 147464 | tf_op jit(solution)/shard_map/ppermute | solution.py:18
  9.6 3.4 %collective-permute-start.1 = (f32[1,6,2048]{2,1,0:T(8,128)}, f32[1,6,2048]{2,1,0:T(8,128)S(1)}, u32[]{:S(2)}, u32[]{:S(2)}) collective-permute-start(f32[1,6,2048]{2,1,0:T(8,128)} %bitcast.90), channel_id=1, source_target_pairs={{16,0},{17,1},{18,2},{19,3},{20,4},{21,5},{22,6},{23,7},{24,8},{25... | collective-permute-start | bytes 147464 | tf_op jit(solution)/shard_map/ppermute | solution.py:20
  13.8 255.0 %copy-start.1 = (f32[21]{0:T(128)S(1)}, f32[21]{0:T(128)}, u32[]{:S(2)}) copy-start(f32[21]{0:T(128)} %constant.22.clone) | copy-start | bytes 256
  159.2 0.7 copy-start
Sparse Core Ops, SparseCore 0:
  160.0 108.7 all-reduce.1
where the time goes:
time: 280 us; the launch traced here: 279 us
  waiting for transfers between devices  110 us (39%)
  other arithmetic  88.2 us (32%)
  matrix products  50.4 us (18%)
  between operations  14.1 us (5%)
  local copies, waits for them, and re-layouts  12 us (4%)
  starting transfers between devices  3.73 us (1%)
    psum x1, waiting for transfers between devices, shards(): whole = lax.psum(partial_gram, 'blk')  109 us
    dot_general x4, other arithmetic, accumulate(): lax.dot_general(extended, mixing, (((1,), (1,)), ((), ())), precision=lax...  85.7 us
    dot_general x4, matrix products, accumulate(): lax.dot_general(extended, mixing, (((1,), (1,)), ((), ())), precision=lax...  45.7 us
  transfers between devices with their start and end apart: 3, of which 2 were waited for; matrix products, arithmetic and copies ran while one was open for 0% of the time, Pallas kernels for 0%

commit v1 on v0

--- a/solution.py
+++ b/solution.py
@@ -97,7 +97,10 @@
     partial_gram, _ = lax.scan(
         accumulate, start_total, (null_blocks, index_blocks, weight_blocks, id_blocks)
     )
-    whole = lax.psum(partial_gram, "blk")
+    press_the_ranges = lambda local_block, axis_tag: lax.all_gather(
+        local_block, axis_name=axis_tag
+    ).sum(axis=0)
+    whole = press_the_ranges(partial_gram, axis_tag="blk")
     offset = lax.axis_index("blk") * AGG_DEV
     mine = lax.dynamic_slice_in_dim(whole, offset, AGG_DEV, 1)
     identity = jnp.array([1.0 if p == q else 0.0 for p, q in pairs], jnp.float32)

time: 280 us -> 237 us (0.85)
  waiting for transfers between devices: 110 us -> 65.8 us
    psum x1 -> x0, waiting for transfers between devices: 109 us -> none  [shards(): whole = lax.psum(partial_gram, 'blk')]
    all_gather x0 -> x1, waiting for transfers between devices: none -> 64.4 us  [shards(): lax.all_gather(local_block, axis_name=axis_tag).sum(axis=0)]
where the time goes in v1:
time: 237 us; the launch traced here: 236 us
  other arithmetic  89.3 us (38%)
  waiting for transfers between devices  65.8 us (28%)
  matrix products  50.4 us (21%)
  between operations  14.1 us (6%)
  local copies, waits for them, and re-layouts  12.2 us (5%)
  starting transfers between devices  3.73 us (2%)
    dot_general x4, other arithmetic, accumulate(): lax.dot_general(extended, mixing, (((1,), (1,)), ((), ())), precision=lax...  85.7 us
    all_gather x1, waiting for transfers between devices, shards(): lax.all_gather(local_block, axis_name=axis_tag).sum(axis=0)  64.4 us
    dot_general x4, matrix products, accumulate(): lax.dot_general(extended, mixing, (((1,), (1,)), ((), ())), precision=lax...  45.7 us
  transfers between devices with their start and end apart: 3, of which 2 were waited for; matrix products, arithmetic and copies ran while one was open for 0% of the time, Pallas kernels for 0%

profile of v1, /device:TPU:0, one launch (start us, length us, event | category | flops | bytes accessed | tf_op | source)
XLA Modules:
  0.0 235.7 jit_solution(7281623664416244246)
XLA Ops:
  7.2 0.0 all-gather.4.cloned.1.call-start
  7.2 2.4 %collective-permute-start = (f32[1,6,2048]{2,1,0:T(8,128)}, f32[1,6,2048]{2,1,0:T(8,128)S(1)}, u32[]{:S(2)}, u32[]{:S(2)}) collective-permute-start(f32[1,6,2048]{2,1,0:T(8,128)} %bitcast.90), channel_id=1, source_target_pairs={{0,16},{1,17},{2,18},{3,19},{4,20},{5,21},{6,22},{7,23},{8,24},{9,... | collective-permute-start | bytes 147464 | tf_op jit(solution)/shard_map/ppermute | solution.py:18
  9.6 1.3 collective-permute-start.1
  10.9 0.7 reshape.96
  11.6 0.0 collective-permute-done
  11.6 1.3 collective-permute-done.1
  13.0 0.9 pad_maximum_fusion
  13.8 0.0 copy-start.1
  13.9 145.5 %while.12 = (s32[]{:T(128)}, f32[21,1536]{1,0:T(8,128)S(1)}, f32[4,6,512]{2,1,0:T(8,128)}, s32[4,8,512]{2,1,0:T(8,128)}, f32[4,8,512]{2,1,0:T(8,128)}, /*index=5...) while((s32[]{:T(128)}, f32[21,1536]{1,0:T(8,128)S(1)}, ...), condition=%wide.region_1.2_spmd.clone.clone, body=%wide.region_0.1_spmd.clone.clone.sunk | while | flops 497889792 | bytes 25895224 | solution.py:97
  13.9 1.0 constant_dynamic-slice_fusion.20
  14.9 1.0 constant_dynamic-slice_fusion.21
  16.0 21.4 %fusion.81 = f32[512,6144]{1,0:T(8,128)S(1)} fusion(f32[512]{0:T(512)S(1)} %bitcast.101, s32[512]{0:T(512)S(1)} %bitcast.109, f32[512]{0:T(512)S(1)} %bitcast.95, s32[512]{0:T(512)S(1)} %bitcast.103, f32[512]{0:T(512)S(1)} %bitcast.96, s32[512]{0:T(512)S(1)} %bitcast.104, f32[512]{0:T(512)S(1)} %bitcast.97, ...), kind=kLoop, calls=%fused_computation.11.clone.clone.clone.clone.clone.1.clone.1 | loop fusion | flops 72351744 | bytes 12615680 | tf_op jit(solution)/shard_map/while/body/eval_jaxpr/dot_general | solution.py:81
  37.4 11.4 %fusion.82 = f32[6,512]{1,0:T(8,128)S(1)} fusion(f32[6,6144]{1,0:T(8,128)S(1)} %get-tuple-element.373, f32[4,6,512]{2,1,0:T(8,128)} %get-tuple-element.370, s32[]{:T(128)} %get-tuple-element.352, f32[512,6144]{1,0:T(8,128)S(1)} %fusion.81), kind=kOutput, calls=%fused_computation.48.clone.2 | convolution fusion | flops 226495488 | bytes 12754948 | tf_op jit(solution)/shard_map/while/body/eval_jaxpr/dot_general | solution.py:81
  48.9 0.1 stack.8
  49.0 1.2 fusion.83
  50.2 1.0 constant_dynamic-slice_fusion.20
  51.2 1.0 constant_dynamic-slice_fusion.21
  52.3 21.4 %fusion.81 = f32[512,6144]{1,0:T(8,128)S(1)} fusion(f32[512]{0:T(512)S(1)} %bitcast.101, s32[512]{0:T(512)S(1)} %bitcast.109, f32[512]{0:T(512)S(1)} %bitcast.95, s32[512]{0:T(512)S(1)} %bitcast.103, f32[512]{0:T(512)S(1)} %bitcast.96, s32[512]{0:T(512)S(1)} %bitcast.104, f32[512]{0:T(512)S(1)} %bitcast.97, ...), kind=kLoop, calls=%fused_computation.11.clone.clone.clone.clone.clone.1.clone.1 | loop fusion | flops 72351744 | bytes 12615680 | tf_op jit(solution)/shard_map/while/body/eval_jaxpr/dot_general | solution.py:81
  73.7 11.4 %fusion.82 = f32[6,512]{1,0:T(8,128)S(1)} fusion(f32[6,6144]{1,0:T(8,128)S(1)} %get-tuple-element.373, f32[4,6,512]{2,1,0:T(8,128)} %get-tuple-element.370, s32[]{:T(128)} %get-tuple-element.352, f32[512,6144]{1,0:T(8,128)S(1)} %fusion.81), kind=kOutput, calls=%fused_computation.48.clone.2 | convolution fusion | flops 226495488 | bytes 12754948 | tf_op jit(solution)/shard_map/while/body/eval_jaxpr/dot_general | solution.py:81
  85.2 0.1 stack.8
  85.3 1.2 fusion.83
  86.5 1.0 constant_dynamic-slice_fusion.20
  87.6 1.0 constant_dynamic-slice_fusion.21
  88.6 21.4 %fusion.81 = f32[512,6144]{1,0:T(8,128)S(1)} fusion(f32[512]{0:T(512)S(1)} %bitcast.101, s32[512]{0:T(512)S(1)} %bitcast.109, f32[512]{0:T(512)S(1)} %bitcast.95, s32[512]{0:T(512)S(1)} %bitcast.103, f32[512]{0:T(512)S(1)} %bitcast.96, s32[512]{0:T(512)S(1)} %bitcast.104, f32[512]{0:T(512)S(1)} %bitcast.97, ...), kind=kLoop, calls=%fused_computation.11.clone.clone.clone.clone.clone.1.clone.1 | loop fusion | flops 72351744 | bytes 12615680 | tf_op jit(solution)/shard_map/while/body/eval_jaxpr/dot_general | solution.py:81
  110.0 11.4 %fusion.82 = f32[6,512]{1,0:T(8,128)S(1)} fusion(f32[6,6144]{1,0:T(8,128)S(1)} %get-tuple-element.373, f32[4,6,512]{2,1,0:T(8,128)} %get-tuple-element.370, s32[]{:T(128)} %get-tuple-element.352, f32[512,6144]{1,0:T(8,128)S(1)} %fusion.81), kind=kOutput, calls=%fused_computation.48.clone.2 | convolution fusion | flops 226495488 | bytes 12754948 | tf_op jit(solution)/shard_map/while/body/eval_jaxpr/dot_general | solution.py:81
  121.5 0.1 stack.8
  121.7 1.2 fusion.83
  122.9 1.0 constant_dynamic-slice_fusion.20
  123.9 1.2 constant_dynamic-slice_fusion.21
  125.1 21.4 %fusion.81 = f32[512,6144]{1,0:T(8,128)S(1)} fusion(f32[512]{0:T(512)S(1)} %bitcast.101, s32[512]{0:T(512)S(1)} %bitcast.109, f32[512]{0:T(512)S(1)} %bitcast.95, s32[512]{0:T(512)S(1)} %bitcast.103, f32[512]{0:T(512)S(1)} %bitcast.96, s32[512]{0:T(512)S(1)} %bitcast.104, f32[512]{0:T(512)S(1)} %bitcast.97, ...), kind=kLoop, calls=%fused_computation.11.clone.clone.clone.clone.clone.1.clone.1 | loop fusion | flops 72351744 | bytes 12615680 | tf_op jit(solution)/shard_map/while/body/eval_jaxpr/dot_general | solution.py:81
  146.5 11.4 %fusion.82 = f32[6,512]{1,0:T(8,128)S(1)} fusion(f32[6,6144]{1,0:T(8,128)S(1)} %get-tuple-element.373, f32[4,6,512]{2,1,0:T(8,128)} %get-tuple-element.370, s32[]{:T(128)} %get-tuple-element.352, f32[512,6144]{1,0:T(8,128)S(1)} %fusion.81), kind=kOutput, calls=%fused_computation.48.clone.2 | convolution fusion | flops 226495488 | bytes 12754948 | tf_op jit(solution)/shard_map/while/body/eval_jaxpr/dot_general | solution.py:81
  158.0 0.1 stack.8
  158.2 1.2 fusion.83
  159.3 0.0 copy-start
  159.4 0.6 copy-done
  160.0 0.0 all-gather.4.cloned.1.call-update
  160.0 64.4 %all-gather.4.cloned.1.call-done = f32[16,21,1536]{2,1,0:T(8,128)} async-done(((f32[1,21,1536]{2,1,0:T(8,128)}), f32[16,21,1536]{2,1,0:T(8,128)}) %all-gather.4.cloned.1.call-update) | async-done | bytes 2064400 | tf_op jit(solution)/shard_map/all_gather | solution.py:100
  224.4 1.8 reduce_sum.9
  226.2 0.0 copy-done.1
  226.3 0.1 multiply_add_fusion
  226.4 0.6 subtract_bitcast_fusion
  227.0 1.8 stack.4
  (17 shorter events, 0.3 us)
Async XLA Ops:
  7.2 217.3 %all-gather.4.cloned.1.call-start = ((), (), s32[]{:S(2)}) async-start(), calls=%async_computation | async-start | bytes 2506752 | tf_op jit(solution)/shard_map/all_gather | solution.py:100
  7.2 4.4 %collective-permute-start = (f32[1,6,2048]{2,1,0:T(8,128)}, f32[1,6,2048]{2,1,0:T(8,128)S(1)}, u32[]{:S(2)}, u32[]{:S(2)}) collective-permute-start(f32[1,6,2048]{2,1,0:T(8,128)} %bitcast.90), channel_id=1, source_target_pairs={{0,16},{1,17},{2,18},{3,19},{4,20},{5,21},{6,22},{7,23},{8,24},{9,... | collective-permute-start | bytes 147464 | tf_op jit(solution)/shard_map/ppermute | solution.py:18
  9.6 3.4 %collective-permute-start.1 = (f32[1,6,2048]{2,1,0:T(8,128)}, f32[1,6,2048]{2,1,0:T(8,128)S(1)}, u32[]{:S(2)}, u32[]{:S(2)}) collective-permute-start(f32[1,6,2048]{2,1,0:T(8,128)} %bitcast.91), channel_id=1, source_target_pairs={{16,0},{17,1},{18,2},{19,3},{20,4},{21,5},{22,6},{23,7},{24,8},{25... | collective-permute-start | bytes 147464 | tf_op jit(solution)/shard_map/ppermute | solution.py:20
  13.8 212.4 %copy-start.1 = (f32[21]{0:T(128)S(1)}, f32[21]{0:T(128)}, u32[]{:S(2)}) copy-start(f32[21]{0:T(128)} %constant.13.clone) | copy-start | bytes 256
  159.3 0.6 copy-start
Sparse Core Ops, SparseCore 0:
  160.1 64.2 all-gather.3
